TPU v7x, 32 devices: a whole 2x2x4 slice. The times are simulated.
32 devices in a mesh: chars: 2 (over x), prow: 16 (over z, y, core).
Axes of the slice: x: 2, y: 2, z: 4, core: 2. Of those that a mesh axis runs over, the one named last changes fastest.
Arguments:
- queries: bfloat16 [8192, 512], P(('chars', 'prow')), parts along dimension 0, may hold values from -8 to 8
- keys: bfloat16 [8192, 512], P(('chars', 'prow')), parts along dimension 0, may hold values from -8 to 8
- values: bfloat16 [8192, 512], P(('chars', 'prow')), parts along dimension 0, may hold values from -6 to 6
- out_grad: bfloat16 [8192, 512], P(('chars', 'prow')), parts along dimension 0, may hold values from -6 to 6
- valid_counts: int32 [32, 4], P('chars'), parts along dimension 0, may hold values from 1 to 64
- landmark_cols: int32 [32], P('chars'), parts along dimension 0, may hold values from 0 to 3
- landmark_rows: int32 [32, 4], P(('chars', 'prow')), parts along dimension 0, may hold values from 0 to 15, as said below
Outputs:
- attn_out: bfloat16 [8192, 512], P(('chars', 'prow')), parts along dimension 0
- query_grad: bfloat16 [8192, 512], P(('chars', 'prow')), parts along dimension 0
- key_grad: bfloat16 [8192, 512], P(('chars', 'prow')), parts along dimension 0
- value_grad: bfloat16 [8192, 512], P(('chars', 'prow')), parts along dimension 0
There are 2 independent parts, one for each index of `chars`. A program takes and returns all parts, laid end to end along the dimension named above; each array names one. Nothing has to cross between parts.
Inputs may be any that keep to these rules, and one draw needn't show every extreme that they name: `landmark_rows`: the 4 entries of each row are distinct.
All inputs are finite; a program needn't handle non-finite values.
Results may differ from a plain program's by a relative error of at most 0.012.
The roundings to bfloat16 on the way count: a program that leaves them out, or rounds other values in their place, can miss the bound.
Values may be sent and summed in bfloat16 or wider, within the bound.
A program may use at most 192 MiB of HBM per device.

v0:
```python
import math
import jax
import jax.numpy as jnp
from jax import lax
from jax.sharding import PartitionSpec as P

HEADS = 8
HD = 64
BLK = 64
NLAND = 4
PC = 4
masked_score = -1e30


def extended(x, sides, width):
    for axis, dim in sides:
        devices, length = (lax.axis_size(axis), x.shape[dim])
        up = [(i, (i + 1) % devices) for i in range(devices - 1)]
        down = [(j, i) for i, j in up]
        last = lax.slice_in_dim(x, length - width, length, axis=dim)
        first = lax.slice_in_dim(x, 0, width, axis=dim)
        before = lax.ppermute(last, axis, up)
        after = lax.ppermute(first, axis, down)
        x = jnp.concatenate([before, x, after], axis=dim)
    return x


def passed_along(block, axis, distance):
    devices = range(lax.axis_size(axis))
    route = [(i - distance, i) for i in devices if i - distance in devices]
    return lax.ppermute(block, axis, route)


def product(form, left, right):
    return jnp.einsum(form, left, right, preferred_element_type=jnp.float32)


def window_stack(near_rows, columns):
    pieces = [
        near_rows[row_off, col_off : col_off + columns]
        for row_off in range(3)
        for col_off in range(3)
    ]
    stacked = jnp.stack(pieces, axis=1)
    return stacked.reshape(columns, 9 * stacked.shape[2], stacked.shape[3])


def window_mask(count_near, columns, block_len):
    pieces = [
        count_near[row_off, col_off : col_off + columns]
        for row_off in range(3)
        for col_off in range(3)
    ]
    counts = jnp.stack(pieces, axis=1)
    position = jnp.arange(block_len)
    return (position[None, None, :] < counts[:, :, None]).reshape(columns, 9 * block_len)


def spread(grad_window, columns, block_len):
    pieces = grad_window.reshape(columns, 9, block_len, grad_window.shape[-1])
    layers = []
    for row_off in range(3):
        left = jnp.pad(pieces[:, row_off * 3], ((0, 2), (0, 0), (0, 0)))
        middle = jnp.pad(pieces[:, row_off * 3 + 1], ((1, 1), (0, 0), (0, 0)))
        right = jnp.pad(pieces[:, row_off * 3 + 2], ((2, 0), (0, 0), (0, 0)))
        layers.append(left + middle + right)
    return jnp.stack(layers)


def attend(
    query_blocks,
    grad_raw,
    keys_win,
    values_win,
    mask_win,
    keys_land,
    values_land,
    mask_land,
    query_valid,
):
    score_scale = 1.0 / math.sqrt(query_blocks.shape[-1])
    scores_win = product("cqhe,cwhe->chqw", query_blocks, keys_win) * score_scale
    scores_land = product("cqhe,lhe->chql", query_blocks, keys_land) * score_scale
    scores_win = jnp.where(mask_win[:, None, None, :], scores_win, masked_score)
    scores_land = jnp.where(mask_land[None, None, None, :], scores_land, masked_score)
    row_max = jnp.maximum(jnp.max(scores_win, axis=-1), jnp.max(scores_land, axis=-1))
    exp_total = jnp.sum(jnp.exp(scores_win - row_max[..., None]), axis=-1) + jnp.sum(
        jnp.exp(scores_land - row_max[..., None]), axis=-1
    )
    log_total = row_max + jnp.log(exp_total)
    probs_win = jnp.exp(scores_win - log_total[..., None])
    probs_land = jnp.exp(scores_land - log_total[..., None])
    low_win = probs_win.astype(jnp.bfloat16)
    low_land = probs_land.astype(jnp.bfloat16)
    mixed_out = product("chqw,cwhe->cqhe", low_win, values_win) + product(
        "chql,lhe->cqhe", low_land, values_land
    )
    query_mask = query_valid[:, :, None, None]
    attn_part = jnp.where(query_mask, mixed_out, 0.0).astype(jnp.bfloat16)
    grad_in = jnp.where(query_mask, grad_raw, jnp.zeros_like(grad_raw))
    row_delta = jnp.sum(grad_in.astype(jnp.float32) * mixed_out, axis=-1)
    row_delta = jnp.transpose(row_delta, (0, 2, 1))[..., None]
    dprob_win = product("cqhe,cwhe->chqw", grad_in, values_win)
    dprob_land = product("cqhe,lhe->chql", grad_in, values_land)
    dscore_win = (probs_win * (dprob_win - row_delta) * score_scale).astype(jnp.bfloat16)
    dscore_land = (probs_land * (dprob_land - row_delta) * score_scale).astype(jnp.bfloat16)
    query_part = (
        product("chqw,cwhe->cqhe", dscore_win, keys_win)
        + product("chql,lhe->cqhe", dscore_land, keys_land)
    ).astype(jnp.bfloat16)
    kgrad_win = product("chqw,cqhe->cwhe", dscore_win, query_blocks)
    vgrad_win = product("chqw,cqhe->cwhe", low_win, grad_in)
    kgrad_land = product("chql,cqhe->lhe", dscore_land, query_blocks)
    vgrad_land = product("chql,cqhe->lhe", low_land, grad_in)
    return (attn_part, query_part, kgrad_win, vgrad_win, kgrad_land, vgrad_land)


def per_device(queries, keys, values, out_grad, valid_counts, landmark_cols, landmark_rows):
    model_width = HEADS * HD
    my_row = lax.axis_index("prow")
    row_total = lax.axis_size("prow")
    position = jnp.arange(BLK)
    key_value = jnp.concatenate([keys, values], axis=1).reshape(1, PC, BLK, 2 * model_width)
    near_rows = extended(key_value, (("prow", 0),), 1)
    near_rows = jnp.pad(near_rows, ((0, 0), (1, 1), (0, 0), (0, 0)))
    count_padded = jnp.pad(valid_counts, ((1, 1), (1, 1)))
    count_near = lax.dynamic_slice_in_dim(count_padded, my_row, 3, 0)
    own_col = lax.dynamic_index_in_dim(landmark_cols, my_row, 0, keepdims=False)
    own_block = lax.dynamic_slice_in_dim(key_value[0], own_col, 1, 0)
    land_panel = lax.all_gather(own_block, "prow", axis=0, tiled=True)
    chosen_rows = landmark_rows[0]
    chosen = jnp.take(land_panel, chosen_rows, axis=0)
    chosen_counts = valid_counts[chosen_rows, landmark_cols[chosen_rows]]
    stacked = window_stack(near_rows, PC)
    keys_win = stacked[..., :model_width].reshape(PC, 9 * BLK, HEADS, HD)
    values_win = stacked[..., model_width:].reshape(PC, 9 * BLK, HEADS, HD)
    mask_win = window_mask(count_near, PC, BLK)
    keys_land = chosen[..., :model_width].reshape(NLAND * BLK, HEADS, HD)
    values_land = chosen[..., model_width:].reshape(NLAND * BLK, HEADS, HD)
    mask_land = (position[None, :] < chosen_counts[:, None]).reshape(NLAND * BLK)
    row_counts = lax.dynamic_index_in_dim(valid_counts, my_row, 0, keepdims=False)
    query_valid = position[None, :] < row_counts[:, None]
    attn_part, query_part, kgrad_win, vgrad_win, kgrad_land, vgrad_land = attend(
        queries.reshape(PC, BLK, HEADS, HD),
        out_grad.reshape(PC, BLK, HEADS, HD),
        keys_win,
        values_win,
        mask_win,
        keys_land,
        values_land,
        mask_land,
        query_valid,
    )
    grad_window = jnp.concatenate(
        [kgrad_win.reshape(PC, 9 * BLK, model_width), vgrad_win.reshape(PC, 9 * BLK, model_width)],
        axis=-1,
    )
    summed = spread(grad_window, PC, BLK)
    own_grads = summed[1, 1 : PC + 1]
    from_above = passed_along(summed[2, 1 : PC + 1], "prow", 1)
    from_below = passed_along(summed[0, 1 : PC + 1], "prow", -1)
    grad_land = jnp.concatenate(
        [kgrad_land.reshape(NLAND, BLK, model_width), vgrad_land.reshape(NLAND, BLK, model_width)],
        axis=-1,
    )
    slot_grads = (
        jnp.zeros((row_total, BLK, 2 * model_width), jnp.float32).at[chosen_rows].add(grad_land)
    )
    land_total = lax.psum_scatter(slot_grads, "prow", scatter_dimension=0, tiled=True)[0]
    hit_mask = (jnp.arange(PC) == own_col)[:, None, None]
    all_grads = own_grads + from_above + from_below + jnp.where(hit_mask, land_total[None], 0.0)
    attn_out = attn_part.reshape(PC * BLK, model_width)
    query_grad = query_part.reshape(PC * BLK, model_width)
    key_grad = all_grads[..., :model_width].astype(jnp.bfloat16).reshape(PC * BLK, model_width)
    value_grad = all_grads[..., model_width:].astype(jnp.bfloat16).reshape(PC * BLK, model_width)
    return (attn_out, query_grad, key_grad, value_grad)


def solution(mesh):
    return jax.shard_map(
        per_device,
        mesh=mesh,
        in_specs=(
            P(("chars", "prow"), None),
            P(("chars", "prow"), None),
            P(("chars", "prow"), None),
            P(("chars", "prow"), None),
            P("chars", None),
            P("chars"),
            P(("chars", "prow"), None),
        ),
        out_specs=(
            P(("chars", "prow"), None),
            P(("chars", "prow"), None),
            P(("chars", "prow"), None),
            P(("chars", "prow"), None),
        ),
        check_vma=False,
    )
```

profile of v0, /device:TPU:1, one launch (start us, length us, event | category | flops | bytes accessed | tf_op | source)
XLA Modules:
  0.0 191.7 jit_solution(16934145135606755180)
XLA Ops:
  11.2 4.5 %collective-permute-start = (bf16[1,4,64,1024]{3,2,1,0:T(8,128)(2,1)S(1)}, bf16[1,4,64,1024]{3,2,1,0:T(8,128)(2,1)S(1)}, u32[]{:S(2)}, u32[]{:S(2)}) collective-permute-start(bf16[1,4,64,1024]{3,2,1,0:T(8,128)(2,1)S(1)} %bitcast.261), channel_id=1, source_target_pairs={{0,1},{1,2},{2,3},{3,4},{4,5},{5,6},{6,7},{7,8},{8,9},{9,10},{10,1... | collective-permute-start | bytes 1572872 | tf_op jit(solution)/shard_map/ppermute | solution.py:22
  32.3 2.6 %copy.132 = bf16[4,576,512]{1,2,0:T(8,128)(2,1)} copy(bf16[4,576,512]{2,1,0:T(8,128)(2,1)S(1)} %get-tuple-element.15) | data formatting | bytes 4718592 | tf_op jit(solution)/shard_map/slice | solution.py:136
  34.8 3.1 %copy.142 = bf16[4,576,512]{1,2,0:T(8,128)(2,1)S(1)} copy(bf16[4,576,512]{2,1,0:T(8,128)(2,1)} %get-tuple-element.16) | data formatting | bytes 4718592 | tf_op jit(solution)/shard_map/slice | solution.py:135
  38.0 3.3 %bitcast_reduce_fusion = (f32[4,8,64]{2,1,0:T(8,128)S(1)}, f32[4,8,576,64]{2,3,1,0:T(8,128)}) fusion(pred[4,576]{1,0:T(4,128)(4,1)S(1)} %broadcast_compare_fusion, bf16[4,64,8,64]{1,3,2,0:T(8,128)(2,1)S(1)} %copy.161, bf16[4,576,8,64]{1,3,2,0:T(8,128)(2,1)S(1)} %bitcast.256), kind=kOutput, calls=%fused_computation.8 | convolution fusion | flops 154531840 | bytes 7350528 | tf_op jit(solution)/shard_map/cqhe,cwhe->chqw/dot_general | solution.py:35
  41.3 20.8 %all-gather.2.cloned.1.call-done = bf16[16,64,1024]{2,1,0:T(8,128)(2,1)} async-done(((bf16[1,64,1024]{2,1,0:T(8,128)(2,1)}), bf16[16,64,1024]{2,1,0:T(8,128)(2,1)}) %all-gather.2.cloned.1.call-update) | async-done | bytes 2097168 | tf_op jit(solution)/shard_map/all_gather | solution.py:130
  62.1 2.2 %gather_fusion.2 = bf16[4,64,1024]{2,1,0:T(8,128)(2,1)S(1)} fusion(bf16[16,64,1024]{2,1,0:T(8,128)(2,1)} %all-gather.2.cloned.1.call-done, s32[1024]{0:T(1024)S(1)} %pad_clamp_fusion), kind=kCustom, calls=%fused_computation.2 | custom fusion | bytes 1048592 | tf_op jit(solution)/shard_map/jit(_take)/gather | solution.py:132
  72.0 2.4 %select_convert_fusion = (bf16[4,64,8,64]{1,3,2,0:T(8,128)(2,1)}, f32[4,64,8,64]{1,3,2,0:T(8,128)S(1)}) fusion(pred[4,64]{1,0:T(4,128)(4,1)S(1)} %iota_compare_fusion.3, f32[4,64,8,64]{1,3,2,0:T(8,128)S(1)} %convolution_bitcast_fusion.4, bf16[4,576,8,64]{1,3,2,0:T(8,128)(2,1)S(1)} %bitcast.266, f32[4,8,576,64]{2,3,1,0:T(8,128)S(1)} %copy-done, ...), kind=kOutput, calls=%fused_computation.63 | convolution fusion | flops 155975680 | bytes 8399360 | tf_op jit(solution)/shard_map/chqw,cwhe->cqhe/dot_general | solution.py:35
  77.2 2.5 %reshape.234 = f32[4,64,512]{1,0,2:T(4,128)} reshape(f32[256,8,64]{0,2,1:T(8,128)} %convolution_bitcast_fusion.7) | data formatting | bytes 1048576 | tf_op jit(solution)/shard_map/reshape | solution.py:163
  79.7 2.4 %copy.179 = f32[4,64,512]{2,1,0:T(8,128)} copy(f32[4,64,512]{1,0,2:T(4,128)} %reshape.234) | data formatting | bytes 1048576 | tf_op jit(solution)/shard_map/reshape | solution.py:163
  86.7 2.5 %broadcast_in_dim.107 = f32[16,64,1024]{2,1,0:T(8,128)} broadcast(f32[]{:T(128)} %constant.32.clone.1), dimensions={} | broadcast | bytes 4194308 | tf_op jit(solution)/shard_map/broadcast_in_dim | solution.py:167
  89.2 3.1 %scatter_fusion = f32[16,64,1024]{2,1,0:T(8,128)} fusion(f32[16,64,1024]{2,1,0:T(8,128)} %broadcast_in_dim.107, s32[4]{0:T(128)S(1)} %fusion.44, f32[4,64,1024]{2,1,0:T(8,128)S(1)} %pad_maximum_fusion), kind=kCustom, calls=%fused_computation.3 | custom fusion | flops 262144 | bytes 3145744 | tf_op jit(solution)/shard_map/scatter-add | solution.py:167
  93.4 5.3 %multiply_convert_fusion = bf16[4,8,64,576]{3,2,1,0:T(8,128)(2,1)S(1)} fusion(f32[4,8,576,64]{2,3,1,0:T(8,128)} %get-tuple-element.31, f32[4,8,64]{2,1,0:T(8,128)S(1)} %bitcast.273, f32[4,8,64]{2,1,0:T(8,128)S(1)} %fusion.35, pred[4,576]{1,0:T(4,128)(4,1)S(1)} %broadcast_compare_fusion, bf16[4,64,8,64]{1,3,2,0:T(8,128)(2,1)S(1)} %copy-done.9, ...), kind=kOutput, calls=%fused_computation.12 | convolution fusion | flops 159252480 | bytes 9718016 | tf_op jit(solution)/shard_map/cqhe,cwhe->chqw/dot_general | solution.py:35
  100.1 3.1 %convolution_bitcast_fusion = f32[4,576,8,64]{1,3,2,0:T(8,128)} fusion(bf16[4,64,8,64]{1,3,2,0:T(8,128)(2,1)S(1)} %copy.161, bf16[4,8,64,576]{3,2,1,0:T(8,128)(2,1)S(1)} %multiply_convert_fusion), kind=kOutput, calls=%fused_computation.19 | convolution fusion | flops 150994944 | bytes 7340032 | tf_op jit(solution)/shard_map/chqw,cqhe->cwhe/dot_general | solution.py:35
  103.2 8.5 %copy.162 = f32[4,576,8,64]{3,2,1,0:T(8,128)} copy(f32[4,576,8,64]{1,3,2,0:T(8,128)} %convolution_bitcast_fusion) | data formatting | bytes 9437184 | tf_op jit(solution)/shard_map/chqw,cqhe->cwhe/transpose | solution.py:35
  111.7 9.0 %concatenate.23 = f32[4,9,64,512]{3,2,1,0:T(8,128)} reshape(f32[4,576,8,64]{3,2,1,0:T(8,128)} %copy.162) | data formatting | bytes 9437184 | tf_op jit(solution)/shard_map/concatenate | solution.py:154
  120.6 6.1 %convolution_bitcast_fusion.1 = f32[4,576,8,64]{1,3,2,0:T(8,128)} fusion(bf16[4,64,8,64]{1,3,2,0:T(8,128)(2,1)S(1)} %copy-done.9, f32[4,8,576,64]{2,3,1,0:T(8,128)} %get-tuple-element.31, f32[4,8,64]{2,1,0:T(8,128)S(1)} %fusion.35, pred[4,576]{1,0:T(4,128)(4,1)S(1)} %broadcast_compare_fusion), kind=kOutput, calls=%fused_computation.20 | convolution fusion | flops 155713536 | bytes 9709824 | tf_op jit(solution)/shard_map/chqw,cqhe->cwhe/dot_general | solution.py:35
  126.8 8.2 %copy.163 = f32[4,576,8,64]{3,2,1,0:T(8,128)} copy(f32[4,576,8,64]{1,3,2,0:T(8,128)} %convolution_bitcast_fusion.1) | data formatting | bytes 9437184 | tf_op jit(solution)/shard_map/chqw,cqhe->cwhe/transpose | solution.py:35
  135.0 9.0 %concatenate.24 = f32[4,9,64,512]{3,2,1,0:T(8,128)} reshape(f32[4,576,8,64]{3,2,1,0:T(8,128)} %copy.163) | data formatting | bytes 9437184 | tf_op jit(solution)/shard_map/concatenate | solution.py:154
  144.0 3.0 %constant_dynamic-update-slice_fusion.4 = f32[4,9,64,1024]{3,2,1,0:T(8,128)S(1)} fusion(f32[4,9,64,512]{3,2,1,0:T(8,128)} %concatenate.23), kind=kLoop, calls=%fused_computation.88 | loop fusion | bytes 9437184
  148.3 2.8 %slice_bitcast_fusion.11 = (f32[4,64,1024]{2,1,0:T(8,128)}, f32[4,64,1024]{2,1,0:T(8,128)S(1)}, f32[4,64,1024]{2,1,0:T(8,128)S(1)}, f32[4,64,1024]{2,1,0:T(8,128...) fusion(f32[4,9,64,1024]{3,2,1,0:T(8,128)S(1)} %constant_dynamic, ...), kind=kLoop, calls=%fused_computation.59 | loop fusion | bytes 18874368 | tf_op jit(solution)/shard_map/squeeze | solution.py:63
  152.4 2.2 %collective-permute-start.3 = (f32[4,64,1024]{2,1,0:T(8,128)}, f32[4,64,1024]{2,1,0:T(8,128)}, u32[]{:S(2)}, u32[]{:S(2)}) collective-permute-start(f32[4,64,1024]{2,1,0:T(8,128)} %slice_bitcast_fusion), channel_id=1, source_target_pairs={{1,0},{2,1},{3,2},{4,3},{5,4},{6,5},{7,6},{8,7},{9,8},{10,9},{11,1... | collective-permute-start | bytes 3145736 | tf_op jit(solution)/shard_map/ppermute | solution.py:31
  156.0 3.8 %collective-permute-start.2 = (f32[4,64,1024]{2,1,0:T(8,128)}, f32[4,64,1024]{2,1,0:T(8,128)}, u32[]{:S(2)}, u32[]{:S(2)}) collective-permute-start(f32[4,64,1024]{2,1,0:T(8,128)} %slice_bitcast_fusion.4), channel_id=1, source_target_pairs={{0,1},{1,2},{2,3},{3,4},{4,5},{5,6},{6,7},{7,8},{8,9},{9,10},{10,1... | collective-permute-start | bytes 3145736 | tf_op jit(solution)/shard_map/ppermute | solution.py:31
  164.7 2.7 %fusion.16 = bf16[4,64,8,64]{1,3,2,0:T(8,128)(2,1)S(1)} fusion(f32[4,64,8,64]{1,3,2,0:T(8,128)S(1)} %convolution_bitcast_fusion.2, bf16[4,576,8,64]{1,3,2,0:T(8,128)(2,1)S(1)} %bitcast.257, bf16[4,8,64,576]{3,2,1,0:T(8,128)(2,1)} %copy-done.4), kind=kOutput, calls=%fused_computation.41 | convolution fusion | flops 151257088 | bytes 5505024 | tf_op jit(solution)/shard_map/chqw,cwhe->cqhe/dot_general | solution.py:35
  171.0 11.1 %collective-permute-done.2 = f32[4,64,1024]{2,1,0:T(8,128)} collective-permute-done((f32[4,64,1024]{2,1,0:T(8,128)}, f32[4,64,1024]{2,1,0:T(8,128)}, u32[]{:S(2)}, u32[]{:S(2)}) %collective-permute-start.2) | collective-permute-done | bytes 1048608 | tf_op jit(solution)/shard_map/ppermute | solution.py:31
  (120 shorter events, 50.9 us)
Async XLA Ops:
  7.2 18.9 %copy-start.15 = (bf16[256,512]{1,0:T(8,128)(2,1)S(1)}, bf16[256,512]{1,0:T(8,128)(2,1)}, u32[]{:S(2)}) copy-start(bf16[256,512]{1,0:T(8,128)(2,1)} %param.7) | copy-start | bytes 786436
  7.2 54.9 %all-gather.2.cloned.1.call-start = ((), (), s32[]{:S(2)}) async-start(), calls=%async_computation.1 | async-start | bytes 2228224 | tf_op jit(solution)/shard_map/all_gather | solution.py:130
  8.2 19.9 %copy-start.16 = (bf16[256,512]{1,0:T(8,128)(2,1)S(1)}, bf16[256,512]{1,0:T(8,128)(2,1)}, u32[]{:S(2)}) copy-start(bf16[256,512]{1,0:T(8,128)(2,1)} %param.10) | copy-start | bytes 786436
  9.3 20.4 %collective-permute-start.1 = (bf16[1,4,64,1024]{3,2,1,0:T(8,128)(2,1)S(1)}, bf16[1,4,64,1024]{3,2,1,0:T(8,128)(2,1)S(1)}, u32[]{:S(2)}, u32[]{:S(2)}) collective-permute-start(bf16[1,4,64,1024]{3,2,1,0:T(8,128)(2,1)S(1)} %bitcast.260), channel_id=1, source_target_pairs={{1,0},{2,1},{3,2},{4,3},{5,4},{6,5},{7,6},{8,7},{9,8},{10,9},{11,1... | collective-permute-start | bytes 1572872 | tf_op jit(solution)/shard_map/ppermute | solution.py:23
  11.2 18.4 %collective-permute-start = (bf16[1,4,64,1024]{3,2,1,0:T(8,128)(2,1)S(1)}, bf16[1,4,64,1024]{3,2,1,0:T(8,128)(2,1)S(1)}, u32[]{:S(2)}, u32[]{:S(2)}) collective-permute-start(bf16[1,4,64,1024]{3,2,1,0:T(8,128)(2,1)S(1)} %bitcast.261), channel_id=1, source_target_pairs={{0,1},{1,2},{2,3},{3,4},{4,5},{5,6},{6,7},{7,8},{8,9},{9,10},{10,1... | collective-permute-start | bytes 1572872 | tf_op jit(solution)/shard_map/ppermute | solution.py:22
  19.6 162.4 %reduce-scatter.2.cloned.1.call-start = ((), (), s32[]{:S(2)}) async-start(), calls=%async_computation.2 | async-start | bytes 4456448 | tf_op jit(solution)/shard_map/reduce_scatter | solution.py:169
  26.4 3.6 %copy-start.6 = (bf16[4,64,8,64]{3,2,1,0:T(8,128)(2,1)}, bf16[4,64,8,64]{3,2,1,0:T(8,128)(2,1)S(1)}, u32[]{:S(2)}) copy-start(bf16[4,64,8,64]{3,2,1,0:T(8,128)(2,1)S(1)} %reshape.185) | copy-start | bytes 786436
  37.9 3.3 %copy-start.1 = (bf16[4,576,512]{1,2,0:T(8,128)(2,1)}, bf16[4,576,512]{1,2,0:T(8,128)(2,1)S(1)}, u32[]{:S(2)}) copy-start(bf16[4,576,512]{1,2,0:T(8,128)(2,1)S(1)} %copy.142) | copy-start | bytes 7077892
  64.3 2.1 %copy-start.13 = (bf16[4,64,8,64]{3,1,0,2:T(8,128)(2,1)S(1)}, bf16[4,64,8,64]{3,1,0,2:T(8,128)(2,1)}, u32[]{:S(2)}) copy-start(bf16[4,64,8,64]{3,1,0,2:T(8,128)(2,1)} %copy.145) | copy-start | bytes 786436
  66.4 2.5 %copy-start = (f32[4,8,576,64]{2,3,1,0:T(8,128)S(1)}, f32[4,8,576,64]{2,3,1,0:T(8,128)}, u32[]{:S(2)}) copy-start(f32[4,8,576,64]{2,3,1,0:T(8,128)} %get-tuple-element.31) | copy-start | bytes 14155780
  68.9 1.4 copy-start.14
  70.2 1.7 copy-start.10
  72.0 2.4 %copy-start.11 = (bf16[4,64,8,64]{1,3,2,0:T(8,128)(2,1)S(1)}, bf16[4,64,8,64]{1,3,2,0:T(8,128)(2,1)}, u32[]{:S(2)}) copy-start(bf16[4,64,8,64]{1,3,2,0:T(8,128)(2,1)} %copy.153) | copy-start | bytes 786436
  74.6 5.1 %copy-start.8 = (bf16[4,64,8,64]{1,3,2,0:T(8,128)(2,1)}, bf16[4,64,8,64]{1,3,2,0:T(8,128)(2,1)S(1)}, u32[]{:S(2)}) copy-start(bf16[4,64,8,64]{1,3,2,0:T(8,128)(2,1)S(1)} %get-tuple-element.5) | copy-start | bytes 786436
  83.6 1.8 copy-start.7
  84.4 1.0 copy-start.5
  85.4 1.1 copy-start.12
  92.3 1.0 copy-start.9
  98.6 1.5 copy-start.4
  144.0 3.8 %copy-start.3 = (f32[4,9,64,512]{3,2,1,0:T(8,128)S(1)}, f32[4,9,64,512]{3,2,1,0:T(8,128)}, u32[]{:S(2)}) copy-start(f32[4,9,64,512]{3,2,1,0:T(8,128)} %concatenate.24) | copy-start | bytes 14155780
  152.4 18.5 %collective-permute-start.3 = (f32[4,64,1024]{2,1,0:T(8,128)}, f32[4,64,1024]{2,1,0:T(8,128)}, u32[]{:S(2)}, u32[]{:S(2)}) collective-permute-start(f32[4,64,1024]{2,1,0:T(8,128)} %slice_bitcast_fusion), channel_id=1, source_target_pairs={{1,0},{2,1},{3,2},{4,3},{5,4},{6,5},{7,6},{8,7},{9,8},{10,9},{11,1... | collective-permute-start | bytes 3145736 | tf_op jit(solution)/shard_map/ppermute | solution.py:31
  156.0 8.7 %copy-start.2 = (bf16[4,576,512]{1,2,0:T(8,128)(2,1)S(1)}, bf16[4,576,512]{1,2,0:T(8,128)(2,1)}, u32[]{:S(2)}) copy-start(bf16[4,576,512]{1,2,0:T(8,128)(2,1)} %copy-done.1) | copy-start | bytes 7077892
  156.0 26.1 %collective-permute-start.2 = (f32[4,64,1024]{2,1,0:T(8,128)}, f32[4,64,1024]{2,1,0:T(8,128)}, u32[]{:S(2)}, u32[]{:S(2)}) collective-permute-start(f32[4,64,1024]{2,1,0:T(8,128)} %slice_bitcast_fusion.4), channel_id=1, source_target_pairs={{0,1},{1,2},{2,3},{3,4},{4,5},{5,6},{6,7},{7,8},{8,9},{9,10},{10,1... | collective-permute-start | bytes 3145736 | tf_op jit(solution)/shard_map/ppermute | solution.py:31
Sparse Core Ops, SparseCore 0:
  19.7 42.2 all-gather.1
  92.5 70.0 reduce-scatter.1
where the time goes:
time: 193 us; the launch traced here: 192 us
  local copies, waits for them, and re-layouts  86.8 us (45%)
  waiting for transfers between devices  32 us (17%)
  matrix products  29.2 us (15%)
  between operations  16.5 us (9%)
  other arithmetic  14.7 us (8%)
  starting transfers between devices  12.6 us (7%)
    dot_general x10, matrix products, product(): return jnp.einsum(form, left, right, preferred_element_type=jnp.float32)  27.3 us
    all_gather x1, waiting for transfers between devices, per_device(): land_panel = lax.all_gather(own_block, 'prow', axis=0, tiled=True)  20.8 us
    concatenate x3, local copies, waits for them, and re-layouts, per_device(): jnp.concatenate([kgrad_win.reshape(PC, 9 * BLK, model_width), vgrad_win.r...  18.5 us
    transpose x2, local copies, waits for them, and re-layouts, product(): return jnp.einsum(form, left, right, preferred_element_type=jnp.float32)  16.7 us
    ppermute x2, waiting for transfers between devices, passed_along(): return lax.ppermute(block, axis, route)  11.1 us
    unnamed x44, local copies, waits for them, and re-layouts  10.4 us
    ppermute x2, starting transfers between devices, passed_along(): return lax.ppermute(block, axis, route)  6.02 us
    reshape x2, local copies, waits for them, and re-layouts, per_device(): vgrad_land.reshape(NLAND, BLK, model_width)  4.89 us
  transfers between devices with their start and end apart: 6, of which 2 were waited for; matrix products, arithmetic and copies ran while one was open for 48% of the time, Pallas kernels for 0%

commit v1 on v0

--- a/solution.py
+++ b/solution.py
@@ -127,7 +127,25 @@
     count_near = lax.dynamic_slice_in_dim(count_padded, my_row, 3, 0)
     own_col = lax.dynamic_index_in_dim(landmark_cols, my_row, 0, keepdims=False)
     own_block = lax.dynamic_slice_in_dim(key_value[0], own_col, 1, 0)
-    land_panel = lax.all_gather(own_block, "prow", axis=0, tiled=True)
+    size, here, extent = (lax.axis_size("prow"), lax.axis_index("prow"), own_block.shape[0])
+    forward = [(i_2, (i_2 + 1) % size) for i_2 in range(size)]
+    backward = [(i_2, (i_2 - 1) % size) for i_2 in range(size)]
+    land_panel = jnp.zeros(
+        (*own_block.shape[:0], size * extent, *own_block.shape[0 + 1 :]), own_block.dtype
+    )
+    land_panel = lax.dynamic_update_slice_in_dim(land_panel, own_block, here * extent, axis=0)
+    from_left = from_right = own_block
+    middle_2 = size // 2
+    for step in range(1, middle_2 + 1):
+        from_left = lax.ppermute(from_left, "prow", forward)
+        land_panel = lax.dynamic_update_slice_in_dim(
+            land_panel, from_left, (here - step) % size * extent, axis=0
+        )
+        if step < size - middle_2:
+            from_right = lax.ppermute(from_right, "prow", backward)
+            land_panel = lax.dynamic_update_slice_in_dim(
+                land_panel, from_right, (here + step) % size * extent, axis=0
+            )
     chosen_rows = landmark_rows[0]
     chosen = jnp.take(land_panel, chosen_rows, axis=0)
     chosen_counts = valid_counts[chosen_rows, landmark_cols[chosen_rows]]

time: 193 us -> 219 us (1.13)
  starting transfers between devices: 12.6 us -> 45.5 us
  waiting for transfers between devices: 32 us -> 7.41 us
  local copies, waits for them, and re-layouts: 86.8 us -> 101 us
    ppermute x0 -> x15, starting transfers between devices: none -> 28.7 us  [the longest x7 23.8 us: per_device(): from_right = lax.ppermute(from_right, 'prow', backward)]
    all_gather x1 -> x0, waiting for transfers between devices: 20.8 us -> none  [per_device(): land_panel = lax.all_gather(own_block, 'prow', axis=0, tiled=True)]
    dynamic_update_slice x0 -> x16, local copies, waits for them, and re-layouts: none -> 12.3 us  [the longest x8 7.06 us: per_device(): lax.dynamic_update_slice_in_dim(land_panel, from_left, (here - step) % si...]
    ppermute x2, waiting for transfers between devices: 11.1 us -> 2.06 us  [passed_along(): return lax.ppermute(block, axis, route)]
    ppermute x0 -> x15, waiting for transfers between devices: none -> 5.33 us  [the longest x8 5.31 us: per_device(): from_left = lax.ppermute(from_left, 'prow', forward)]
    ppermute x2, starting transfers between devices: 6.02 us -> 10.3 us  [passed_along(): return lax.ppermute(block, axis, route)]
    slice x2, local copies, waits for them, and re-layouts: 4.48 us -> 6.93 us  [per_device(): values_win = stacked[..., model_width:].reshape(PC, 9 * BLK, HEADS, HD)]
    reduce_sum x1, other arithmetic: 1.37 us -> 3.77 us  [attend(): jnp.sum(jnp.exp(scores_win - row_max[..., None]), axis=-1)]
  transfers between devices with their start and end apart: 6 -> 20, of which waited for: 2 -> 2; matrix products, arithmetic and copies ran while one was open for 48% -> 49% of each run, Pallas kernels for 0% -> 0%
where the time goes in v1:
time: 219 us; the launch traced here: 216 us
  local copies, waits for them, and re-layouts  101 us (46%)
  starting transfers between devices  45.5 us (21%)
  matrix products  29.6 us (14%)
  between operations  16.6 us (8%)
  other arithmetic  15.9 us (7%)
  waiting for transfers between devices  7.41 us (3%)
    dot_general x10, matrix products, product(): return jnp.einsum(form, left, right, preferred_element_type=jnp.float32)  27.8 us
    ppermute x7, starting transfers between devices, per_device(): from_right = lax.ppermute(from_right, 'prow', backward)  23.8 us
    concatenate x3, local copies, waits for them, and re-layouts, per_device(): jnp.concatenate([kgrad_win.reshape(PC, 9 * BLK, model_width), vgrad_win.r...  18.6 us
    transpose x2, local copies, waits for them, and re-layouts, product(): return jnp.einsum(form, left, right, preferred_element_type=jnp.float32)  16.6 us
    ppermute x2, starting transfers between devices, passed_along(): return lax.ppermute(block, axis, route)  10.3 us
    unnamed x62, local copies, waits for them, and re-layouts  9.63 us
    dynamic_update_slice x8, local copies, waits for them, and re-layouts, per_device(): lax.dynamic_update_slice_in_dim(land_panel, from_left, (here - step) % si...  7.06 us
    slice x2, local copies, waits for them, and re-layouts, per_device(): values_win = stacked[..., model_width:].reshape(PC, 9 * BLK, HEADS, HD)  6.93 us
  transfers between devices with their start and end apart: 20, of which 2 were waited for; matrix products, arithmetic and copies ran while one was open for 49% of the time, Pallas kernels for 0%

profile of v1, /device:TPU:1, one launch (start us, length us, event | category | flops | bytes accessed | tf_op | source)
XLA Modules:
  0.0 215.8 jit_solution(15527752904727720772)
XLA Ops:
  11.2 4.5 %collective-permute-start = (bf16[1,4,64,1024]{3,2,1,0:T(8,128)(2,1)S(1)}, bf16[1,4,64,1024]{3,2,1,0:T(8,128)(2,1)S(1)}, u32[]{:S(2)}, u32[]{:S(2)}) collective-permute-start(bf16[1,4,64,1024]{3,2,1,0:T(8,128)(2,1)S(1)} %bitcast.263), channel_id=1, source_target_pairs={{0,1},{1,2},{2,3},{3,4},{4,5},{5,6},{6,7},{7,8},{8,9},{9,10},{10,1... | collective-permute-start | bytes 1572872 | tf_op jit(solution)/shard_map/ppermute | solution.py:22
  36.4 3.2 %collective-permute-start.7 = (bf16[1,64,1024]{2,1,0:T(8,128)(2,1)S(1)}, bf16[1,64,1024]{2,1,0:T(8,128)(2,1)S(1)}, u32[]{:S(2)}, u32[]{:S(2)}) collective-permute-start(bf16[1,64,1024]{2,1,0:T(8,128)(2,1)S(1)} %collective-permute-done.5), channel_id=1, source_target_pairs={{0,15},{1,0},{2,1},{3,2},{4,3},{5,4},{6,5},{7,6},{8,7},{9,8},{10,9... | collective-permute-start | bytes 393224 | tf_op jit(solution)/shard_map/ppermute | solution.py:145
  41.5 5.4 %collective-permute-start.9 = (bf16[1,64,1024]{2,1,0:T(8,128)(2,1)S(1)}, bf16[1,64,1024]{2,1,0:T(8,128)(2,1)S(1)}, u32[]{:S(2)}, u32[]{:S(2)}) collective-permute-start(bf16[1,64,1024]{2,1,0:T(8,128)(2,1)S(1)} %collective-permute-done.7), channel_id=1, source_target_pairs={{0,15},{1,0},{2,1},{3,2},{4,3},{5,4},{6,5},{7,6},{8,7},{9,8},{10,9... | collective-permute-start | bytes 393224 | tf_op jit(solution)/shard_map/ppermute | solution.py:145
  49.8 2.6 %fusion.47 = (bf16[4,576,512]{2,1,0:T(8,128)(2,1)}, bf16[4,576,512]{2,1,0:T(8,128)(2,1)}) fusion(bf16[4,576,1024]{2,1,0:T(8,128)(2,1)S(1)} %bitcast.261), kind=kLoop, calls=%fused_computation.141 | loop fusion | bytes 9437184 | tf_op jit(solution)/shard_map/slice | solution.py:154
  52.4 3.1 %copy.142 = bf16[4,576,512]{1,2,0:T(8,128)(2,1)S(1)} copy(bf16[4,576,512]{2,1,0:T(8,128)(2,1)} %get-tuple-element.18) | data formatting | bytes 4718592 | tf_op jit(solution)/shard_map/slice | solution.py:153
  55.5 3.9 %bitcast_reduce_fusion = (f32[4,8,64]{2,1,0:T(8,128)}, f32[4,8,576,64]{2,3,1,0:T(8,128)}) fusion(pred[4,576]{1,0:T(4,128)(4,1)S(1)} %broadcast_compare_fusion, bf16[4,64,8,64]{1,3,2,0:T(8,128)(2,1)S(1)} %copy.161, bf16[4,576,8,64]{1,3,2,0:T(8,128)(2,1)S(1)} %bitcast.258), kind=kOutput, calls=%fused_computation.8 | convolution fusion | flops 154531840 | bytes 7350528 | tf_op jit(solution)/shard_map/cqhe,cwhe->chqw/dot_general | solution.py:35
  59.5 4.5 %collective-permute-start.11 = (bf16[1,64,1024]{2,1,0:T(8,128)(2,1)S(1)}, bf16[1,64,1024]{2,1,0:T(8,128)(2,1)S(1)}, u32[]{:S(2)}, u32[]{:S(2)}) collective-permute-start(bf16[1,64,1024]{2,1,0:T(8,128)(2,1)S(1)} %collective-permute-done.9), channel_id=1, source_target_pairs={{0,15},{1,0},{2,1},{3,2},{4,3},{5,4},{6,5},{7,6},{8,7},{9,8},{10,9... | collective-permute-start | bytes 393224 | tf_op jit(solution)/shard_map/ppermute | solution.py:145
  64.6 4.3 %copy.132 = bf16[4,576,512]{1,2,0:T(8,128)(2,1)} copy(bf16[4,576,512]{2,1,0:T(8,128)(2,1)} %get-tuple-element.17) | data formatting | bytes 4718592 | tf_op jit(solution)/shard_map/slice | solution.py:154
  69.7 4.4 %collective-permute-start.13 = (bf16[1,64,1024]{2,1,0:T(8,128)(2,1)S(1)}, bf16[1,64,1024]{2,1,0:T(8,128)(2,1)S(1)}, u32[]{:S(2)}, u32[]{:S(2)}) collective-permute-start(bf16[1,64,1024]{2,1,0:T(8,128)(2,1)S(1)} %collective-permute-done.11), channel_id=1, source_target_pairs={{0,15},{1,0},{2,1},{3,2},{4,3},{5,4},{6,5},{7,6},{8,7},{9,8},{10,9... | collective-permute-start | bytes 393224 | tf_op jit(solution)/shard_map/ppermute | solution.py:145
  75.5 5.8 %collective-permute-start.15 = (bf16[1,64,1024]{2,1,0:T(8,128)(2,1)S(1)}, bf16[1,64,1024]{2,1,0:T(8,128)(2,1)S(1)}, u32[]{:S(2)}, u32[]{:S(2)}) collective-permute-start(bf16[1,64,1024]{2,1,0:T(8,128)(2,1)S(1)} %collective-permute-done.13), channel_id=1, source_target_pairs={{0,15},{1,0},{2,1},{3,2},{4,3},{5,4},{6,5},{7,6},{8,7},{9,8},{10,9... | collective-permute-start | bytes 393224 | tf_op jit(solution)/shard_map/ppermute | solution.py:145
  83.9 5.3 %collective-permute-done.16 = bf16[1,64,1024]{2,1,0:T(8,128)(2,1)S(1)} collective-permute-done((bf16[1,64,1024]{2,1,0:T(8,128)(2,1)S(1)}, bf16[1,64,1024]{2,1,0:T(8,128)(2,1)S(1)}, u32[]{:S(2)}, u32[]{:S(2)}) %collective-permute-start.16) | collective-permute-done | bytes 131104 | tf_op jit(solution)/shard_map/ppermute | solution.py:140
  95.8 3.8 %fusion.1 = f32[4,8,64]{2,1,0:T(8,128)S(1)} fusion(f32[4,8,576,64]{2,3,1,0:T(8,128)} %get-tuple-element.33, f32[4,8,64]{2,1,0:T(8,128)S(1)} %copy_maximum_fusion, pred[4,576]{1,0:T(4,128)(4,1)S(1)} %broadcast_compare_fusion), kind=kLoop, calls=%fused_computation.10 | loop fusion | flops 4716544 | bytes 4737280 | tf_op jit(solution)/shard_map/reduce_sum | solution.py:87
  118.3 3.2 %scatter_fusion = f32[16,64,1024]{2,1,0:T(8,128)} fusion(f32[16,64,1024]{2,1,0:T(8,128)} %broadcast_in_dim.111, s32[4]{0:T(128)S(1)} %fusion.45, f32[4,64,1024]{2,1,0:T(8,128)S(1)} %pad_maximum_fusion), kind=kCustom, calls=%fused_computation.3 | custom fusion | flops 262144 | bytes 3145744 | tf_op jit(solution)/shard_map/scatter-add | solution.py:185
  122.5 5.3 %multiply_convert_fusion = bf16[4,8,64,576]{3,2,1,0:T(8,128)(2,1)S(1)} fusion(f32[4,8,576,64]{2,3,1,0:T(8,128)} %get-tuple-element.33, f32[4,8,64]{2,1,0:T(8,128)S(1)} %bitcast.275, f32[4,8,64]{2,1,0:T(8,128)S(1)} %fusion.35, pred[4,576]{1,0:T(4,128)(4,1)S(1)} %broadcast_compare_fusion, bf16[4,64,8,64]{1,3,2,0:T(8,128)(2,1)S(1)} %copy-done.10, ...), kind=kOutput, calls=%fused_computation.12 | convolution fusion | flops 159252480 | bytes 9718016 | tf_op jit(solution)/shard_map/cqhe,cwhe->chqw/dot_general | solution.py:35
  129.3 3.1 %convolution_bitcast_fusion = f32[4,576,8,64]{1,3,2,0:T(8,128)} fusion(bf16[4,64,8,64]{1,3,2,0:T(8,128)(2,1)S(1)} %copy.161, bf16[4,8,64,576]{3,2,1,0:T(8,128)(2,1)S(1)} %multiply_convert_fusion), kind=kOutput, calls=%fused_computation.19 | convolution fusion | flops 150994944 | bytes 7340032 | tf_op jit(solution)/shard_map/chqw,cqhe->cwhe/dot_general | solution.py:35
  132.4 8.4 %copy.162 = f32[4,576,8,64]{3,2,1,0:T(8,128)} copy(f32[4,576,8,64]{1,3,2,0:T(8,128)} %convolution_bitcast_fusion) | data formatting | bytes 9437184 | tf_op jit(solution)/shard_map/chqw,cqhe->cwhe/transpose | solution.py:35
  140.8 9.1 %concatenate.23 = f32[4,9,64,512]{3,2,1,0:T(8,128)} reshape(f32[4,576,8,64]{3,2,1,0:T(8,128)} %copy.162) | data formatting | bytes 9437184 | tf_op jit(solution)/shard_map/concatenate | solution.py:172
  150.0 6.1 %convolution_bitcast_fusion.1 = f32[4,576,8,64]{1,3,2,0:T(8,128)} fusion(bf16[4,64,8,64]{1,3,2,0:T(8,128)(2,1)S(1)} %copy-done.10, f32[4,8,576,64]{2,3,1,0:T(8,128)} %get-tuple-element.33, f32[4,8,64]{2,1,0:T(8,128)S(1)} %fusion.35, pred[4,576]{1,0:T(4,128)(4,1)S(1)} %broadcast_compare_fusion), kind=kOutput, calls=%fused_computation.20 | convolution fusion | flops 155713536 | bytes 9709824 | tf_op jit(solution)/shard_map/chqw,cqhe->cwhe/dot_general | solution.py:35
  156.0 8.2 %copy.163 = f32[4,576,8,64]{3,2,1,0:T(8,128)} copy(f32[4,576,8,64]{1,3,2,0:T(8,128)} %convolution_bitcast_fusion.1) | data formatting | bytes 9437184 | tf_op jit(solution)/shard_map/chqw,cqhe->cwhe/transpose | solution.py:35
  164.2 8.9 %concatenate.24 = f32[4,9,64,512]{3,2,1,0:T(8,128)} reshape(f32[4,576,8,64]{3,2,1,0:T(8,128)} %copy.163) | data formatting | bytes 9437184 | tf_op jit(solution)/shard_map/concatenate | solution.py:172
  173.1 3.0 %constant_dynamic-update-slice_fusion.4 = f32[4,9,64,1024]{3,2,1,0:T(8,128)S(1)} fusion(f32[4,9,64,512]{3,2,1,0:T(8,128)} %concatenate.23), kind=kLoop, calls=%fused_computation.88 | loop fusion | bytes 9437184
  177.4 2.9 %slice_bitcast_fusion.11 = (f32[4,64,1024]{2,1,0:T(8,128)}, f32[4,64,1024]{2,1,0:T(8,128)S(1)}, f32[4,64,1024]{2,1,0:T(8,128)S(1)}, f32[4,64,1024]{2,1,0:T(8,128...) fusion(f32[4,9,64,1024]{3,2,1,0:T(8,128)S(1)} %constant_dynamic, ...), kind=kLoop, calls=%fused_computation.59 | loop fusion | bytes 18874368 | tf_op jit(solution)/shard_map/squeeze | solution.py:63
  181.7 8.1 %collective-permute-start.18 = (f32[4,64,1024]{2,1,0:T(8,128)}, f32[4,64,1024]{2,1,0:T(8,128)}, u32[]{:S(2)}, u32[]{:S(2)}) collective-permute-start(f32[4,64,1024]{2,1,0:T(8,128)} %slice_bitcast_fusion), channel_id=1, source_target_pairs={{1,0},{2,1},{3,2},{4,3},{5,4},{6,5},{7,6},{8,7},{9,8},{10,9},{11,1... | collective-permute-start | bytes 3145736 | tf_op jit(solution)/shard_map/ppermute | solution.py:31
  198.2 2.8 %fusion.16 = bf16[4,64,8,64]{1,3,2,0:T(8,128)(2,1)S(1)} fusion(f32[4,64,8,64]{1,3,2,0:T(8,128)S(1)} %convolution_bitcast_fusion.2, bf16[4,576,8,64]{1,3,2,0:T(8,128)(2,1)S(1)} %bitcast.259, bf16[4,8,64,576]{3,2,1,0:T(8,128)(2,1)} %copy-done.5), kind=kOutput, calls=%fused_computation.41 | convolution fusion | flops 151257088 | bytes 5505024 | tf_op jit(solution)/shard_map/chqw,cwhe->cqhe/dot_general | solution.py:35
  (182 shorter events, 79.3 us)
Async XLA Ops:
  7.2 14.5 %copy-start.23 = (s32[1,4]{1,0:T(1,128)S(1)}, s32[1,4]{1,0:T(1,128)}, u32[]{:S(2)}) copy-start(s32[1,4]{1,0:T(1,128)} %param.13) | copy-start | bytes 52
  7.2 15.0 %copy-start.18 = (bf16[256,512]{1,0:T(8,128)(2,1)S(1)}, bf16[256,512]{1,0:T(8,128)(2,1)}, u32[]{:S(2)}) copy-start(bf16[256,512]{1,0:T(8,128)(2,1)} %param.7) | copy-start | bytes 786436
  7.2 199.0 %reduce-scatter.2.cloned.1.call-start = ((), (), s32[]{:S(2)}) async-start(), calls=%async_computation.1 | async-start | bytes 4456448 | tf_op jit(solution)/shard_map/reduce_scatter | solution.py:187
  9.2 39.9 %collective-permute-start.1 = (bf16[1,4,64,1024]{3,2,1,0:T(8,128)(2,1)S(1)}, bf16[1,4,64,1024]{3,2,1,0:T(8,128)(2,1)S(1)}, u32[]{:S(2)}, u32[]{:S(2)}) collective-permute-start(bf16[1,4,64,1024]{3,2,1,0:T(8,128)(2,1)S(1)} %bitcast.262), channel_id=1, source_target_pairs={{1,0},{2,1},{3,2},{4,3},{5,4},{6,5},{7,6},{8,7},{9,8},{10,9},{11,1... | collective-permute-start | bytes 1572872 | tf_op jit(solution)/shard_map/ppermute | solution.py:23
  11.2 37.9 %collective-permute-start = (bf16[1,4,64,1024]{3,2,1,0:T(8,128)(2,1)S(1)}, bf16[1,4,64,1024]{3,2,1,0:T(8,128)(2,1)S(1)}, u32[]{:S(2)}, u32[]{:S(2)}) collective-permute-start(bf16[1,4,64,1024]{3,2,1,0:T(8,128)(2,1)S(1)} %bitcast.263), channel_id=1, source_target_pairs={{0,1},{1,2},{2,3},{3,4},{4,5},{5,6},{6,7},{7,8},{8,9},{9,10},{10,1... | collective-permute-start | bytes 1572872 | tf_op jit(solution)/shard_map/ppermute | solution.py:22
  21.2 8.7 %collective-permute-start.2 = (bf16[1,64,1024]{2,1,0:T(8,128)(2,1)S(1)}, bf16[1,64,1024]{2,1,0:T(8,128)(2,1)}, u32[]{:S(2)}, u32[]{:S(2)}) collective-permute-start(bf16[1,64,1024]{2,1,0:T(8,128)(2,1)S(1)} %get-tuple-element.7), channel_id=1, source_target_pairs={{0,1},{1,2},{2,3},{3,4},{4,5},{5,6},{6,7},{7,8},{8,9},{9,10},{10,1... | collective-permute-start | bytes 393224 | tf_op jit(solution)/shard_map/ppermute | solution.py:140
  21.7 10.1 %collective-permute-start.3 = (bf16[1,64,1024]{2,1,0:T(8,128)(2,1)S(1)}, bf16[1,64,1024]{2,1,0:T(8,128)(2,1)S(1)}, u32[]{:S(2)}, u32[]{:S(2)}) collective-permute-start(bf16[1,64,1024]{2,1,0:T(8,128)(2,1)S(1)} %get-tuple-element.7), channel_id=1, source_target_pairs={{0,15},{1,0},{2,1},{3,2},{4,3},{5,4},{6,5},{7,6},{8,7},{9,8},{10,9... | collective-permute-start | bytes 393224 | tf_op jit(solution)/shard_map/ppermute | solution.py:145
  29.9 4.7 %collective-permute-start.4 = (bf16[1,64,1024]{2,1,0:T(8,128)(2,1)}, bf16[1,64,1024]{2,1,0:T(8,128)(2,1)S(1)}, u32[]{:S(2)}, u32[]{:S(2)}) collective-permute-start(bf16[1,64,1024]{2,1,0:T(8,128)(2,1)} %collective-permute-done.2), channel_id=1, source_target_pairs={{0,1},{1,2},{2,3},{3,4},{4,5},{5,6},{6,7},{7,8},{8,9},{9,10},{10,1... | collective-permute-start | bytes 393224 | tf_op jit(solution)/shard_map/ppermute | solution.py:140
  31.8 4.6 %collective-permute-start.5 = (bf16[1,64,1024]{2,1,0:T(8,128)(2,1)S(1)}, bf16[1,64,1024]{2,1,0:T(8,128)(2,1)S(1)}, u32[]{:S(2)}, u32[]{:S(2)}) collective-permute-start(bf16[1,64,1024]{2,1,0:T(8,128)(2,1)S(1)} %collective-permute-done.3), channel_id=1, source_target_pairs={{0,15},{1,0},{2,1},{3,2},{4,3},{5,4},{6,5},{7,6},{8,7},{9,8},{10,9... | collective-permute-start | bytes 393224 | tf_op jit(solution)/shard_map/ppermute | solution.py:145
  34.6 6.3 %collective-permute-start.6 = (bf16[1,64,1024]{2,1,0:T(8,128)(2,1)S(1)}, bf16[1,64,1024]{2,1,0:T(8,128)(2,1)}, u32[]{:S(2)}, u32[]{:S(2)}) collective-permute-start(bf16[1,64,1024]{2,1,0:T(8,128)(2,1)S(1)} %collective-permute-done.4), channel_id=1, source_target_pairs={{0,1},{1,2},{2,3},{3,4},{4,5},{5,6},{6,7},{7,8},{8,9},{9,10},{10,1... | collective-permute-start | bytes 393224 | tf_op jit(solution)/shard_map/ppermute | solution.py:140
  36.4 5.0 %collective-permute-start.7 = (bf16[1,64,1024]{2,1,0:T(8,128)(2,1)S(1)}, bf16[1,64,1024]{2,1,0:T(8,128)(2,1)S(1)}, u32[]{:S(2)}, u32[]{:S(2)}) collective-permute-start(bf16[1,64,1024]{2,1,0:T(8,128)(2,1)S(1)} %collective-permute-done.5), channel_id=1, source_target_pairs={{0,15},{1,0},{2,1},{3,2},{4,3},{5,4},{6,5},{7,6},{8,7},{9,8},{10,9... | collective-permute-start | bytes 393224 | tf_op jit(solution)/shard_map/ppermute | solution.py:145
  40.9 18.5 %collective-permute-start.8 = (bf16[1,64,1024]{2,1,0:T(8,128)(2,1)}, bf16[1,64,1024]{2,1,0:T(8,128)(2,1)S(1)}, u32[]{:S(2)}, u32[]{:S(2)}) collective-permute-start(bf16[1,64,1024]{2,1,0:T(8,128)(2,1)} %collective-permute-done.6), channel_id=1, source_target_pairs={{0,1},{1,2},{2,3},{3,4},{4,5},{5,6},{6,7},{7,8},{8,9},{9,10},{10,1... | collective-permute-start | bytes 393224 | tf_op jit(solution)/shard_map/ppermute | solution.py:140
  41.5 18.0 %collective-permute-start.9 = (bf16[1,64,1024]{2,1,0:T(8,128)(2,1)S(1)}, bf16[1,64,1024]{2,1,0:T(8,128)(2,1)S(1)}, u32[]{:S(2)}, u32[]{:S(2)}) collective-permute-start(bf16[1,64,1024]{2,1,0:T(8,128)(2,1)S(1)} %collective-permute-done.7), channel_id=1, source_target_pairs={{0,15},{1,0},{2,1},{3,2},{4,3},{5,4},{6,5},{7,6},{8,7},{9,8},{10,9... | collective-permute-start | bytes 393224 | tf_op jit(solution)/shard_map/ppermute | solution.py:145
  59.5 10.2 %collective-permute-start.10 = (bf16[1,64,1024]{2,1,0:T(8,128)(2,1)S(1)}, bf16[1,64,1024]{2,1,0:T(8,128)(2,1)S(1)}, u32[]{:S(2)}, u32[]{:S(2)}) collective-permute-start(bf16[1,64,1024]{2,1,0:T(8,128)(2,1)S(1)} %collective-permute-done.8), channel_id=1, source_target_pairs={{0,1},{1,2},{2,3},{3,4},{4,5},{5,6},{6,7},{7,8},{8,9},{9,10},{10,1... | collective-permute-start | bytes 393224 | tf_op jit(solution)/shard_map/ppermute | solution.py:140
  59.5 10.2 %collective-permute-start.11 = (bf16[1,64,1024]{2,1,0:T(8,128)(2,1)S(1)}, bf16[1,64,1024]{2,1,0:T(8,128)(2,1)S(1)}, u32[]{:S(2)}, u32[]{:S(2)}) collective-permute-start(bf16[1,64,1024]{2,1,0:T(8,128)(2,1)S(1)} %collective-permute-done.9), channel_id=1, source_target_pairs={{0,15},{1,0},{2,1},{3,2},{4,3},{5,4},{6,5},{7,6},{8,7},{9,8},{10,9... | collective-permute-start | bytes 393224 | tf_op jit(solution)/shard_map/ppermute | solution.py:145
  69.0 23.0 %copy-start.21 = (pred[4]{0:T(512)(128)(4,1)S(1)}, pred[4]{0:T(512)(128)(4,1)}, u32[]{:S(2)}) copy-start(pred[4]{0:T(512)(128)(4,1)} %compare_and_fusion) | copy-start | bytes 16
  69.6 5.8 %collective-permute-start.12 = (bf16[1,64,1024]{2,1,0:T(8,128)(2,1)S(1)}, bf16[1,64,1024]{2,1,0:T(8,128)(2,1)S(1)}, u32[]{:S(2)}, u32[]{:S(2)}) collective-permute-start(bf16[1,64,1024]{2,1,0:T(8,128)(2,1)S(1)} %collective-permute-done.10), channel_id=1, source_target_pairs={{0,1},{1,2},{2,3},{3,4},{4,5},{5,6},{6,7},{7,8},{8,9},{9,10},{10,1... | collective-permute-start | bytes 393224 | tf_op jit(solution)/shard_map/ppermute | solution.py:140
  69.7 5.8 %collective-permute-start.13 = (bf16[1,64,1024]{2,1,0:T(8,128)(2,1)S(1)}, bf16[1,64,1024]{2,1,0:T(8,128)(2,1)S(1)}, u32[]{:S(2)}, u32[]{:S(2)}) collective-permute-start(bf16[1,64,1024]{2,1,0:T(8,128)(2,1)S(1)} %collective-permute-done.11), channel_id=1, source_target_pairs={{0,15},{1,0},{2,1},{3,2},{4,3},{5,4},{6,5},{7,6},{8,7},{9,8},{10,9... | collective-permute-start | bytes 393224 | tf_op jit(solution)/shard_map/ppermute | solution.py:145
  75.4 7.1 %collective-permute-start.14 = (bf16[1,64,1024]{2,1,0:T(8,128)(2,1)S(1)}, bf16[1,64,1024]{2,1,0:T(8,128)(2,1)S(1)}, u32[]{:S(2)}, u32[]{:S(2)}) collective-permute-start(bf16[1,64,1024]{2,1,0:T(8,128)(2,1)S(1)} %collective-permute-done.12), channel_id=1, source_target_pairs={{0,1},{1,2},{2,3},{3,4},{4,5},{5,6},{6,7},{7,8},{8,9},{9,10},{10,1... | collective-permute-start | bytes 393224 | tf_op jit(solution)/shard_map/ppermute | solution.py:140
  75.5 7.7 %collective-permute-start.15 = (bf16[1,64,1024]{2,1,0:T(8,128)(2,1)S(1)}, bf16[1,64,1024]{2,1,0:T(8,128)(2,1)S(1)}, u32[]{:S(2)}, u32[]{:S(2)}) collective-permute-start(bf16[1,64,1024]{2,1,0:T(8,128)(2,1)S(1)} %collective-permute-done.13), channel_id=1, source_target_pairs={{0,15},{1,0},{2,1},{3,2},{4,3},{5,4},{6,5},{7,6},{8,7},{9,8},{10,9... | collective-permute-start | bytes 393224 | tf_op jit(solution)/shard_map/ppermute | solution.py:145
  82.5 6.6 %collective-permute-start.16 = (bf16[1,64,1024]{2,1,0:T(8,128)(2,1)S(1)}, bf16[1,64,1024]{2,1,0:T(8,128)(2,1)S(1)}, u32[]{:S(2)}, u32[]{:S(2)}) collective-permute-start(bf16[1,64,1024]{2,1,0:T(8,128)(2,1)S(1)} %collective-permute-done.14), channel_id=1, source_target_pairs={{0,1},{1,2},{2,3},{3,4},{4,5},{5,6},{6,7},{7,8},{8,9},{9,10},{10,1... | collective-permute-start | bytes 393224 | tf_op jit(solution)/shard_map/ppermute | solution.py:140
  181.7 22.4 %collective-permute-start.18 = (f32[4,64,1024]{2,1,0:T(8,128)}, f32[4,64,1024]{2,1,0:T(8,128)}, u32[]{:S(2)}, u32[]{:S(2)}) collective-permute-start(f32[4,64,1024]{2,1,0:T(8,128)} %slice_bitcast_fusion), channel_id=1, source_target_pairs={{1,0},{2,1},{3,2},{4,3},{5,4},{6,5},{7,6},{8,7},{9,8},{10,9},{11,1... | collective-permute-start | bytes 3145736 | tf_op jit(solution)/shard_map/ppermute | solution.py:31
  191.1 7.1 %copy-start.3 = (bf16[4,576,512]{1,2,0:T(8,128)(2,1)S(1)}, bf16[4,576,512]{1,2,0:T(8,128)(2,1)}, u32[]{:S(2)}) copy-start(bf16[4,576,512]{1,2,0:T(8,128)(2,1)} %copy-done.2) | copy-start | bytes 7077892
  191.1 15.1 %collective-permute-start.17 = (f32[4,64,1024]{2,1,0:T(8,128)}, f32[4,64,1024]{2,1,0:T(8,128)}, u32[]{:S(2)}, u32[]{:S(2)}) collective-permute-start(f32[4,64,1024]{2,1,0:T(8,128)} %slice_bitcast_fusion.4), channel_id=1, source_target_pairs={{0,1},{1,2},{2,3},{3,4},{4,5},{5,6},{6,7},{7,8},{8,9},{9,10},{10,1... | collective-permute-start | bytes 3145736 | tf_op jit(solution)/shard_map/ppermute | solution.py:31
  (22 other events, 64.1 us)
Sparse Core Ops, SparseCore 0:
  121.6 80.0 reduce-scatter.1
